TPU v7x, 32 devices: a whole 2x2x4 slice. The times are simulated.
32 devices in a mesh: seq: 8 (over z, x), tp: 4 (over y, core).
Axes of the slice: x: 2, y: 2, z: 4, core: 2. Of those that a mesh axis runs over, the one named last changes fastest.
Arguments:
- tokens_in: bfloat16 [4, 16, 1024], replicated, may hold values from -6 to 6
- key_cache: bfloat16 [16, 2048, 1024], P(None, 'seq', 'tp'), may hold values from -6 to 6
- value_cache: bfloat16 [16, 2048, 1024], P(None, 'seq', 'tp'), may hold values from -6 to 6
- cache_len: int32 [16], replicated, may hold values from 1 to 2048, as said below
- bucket_table: int32 [2052], replicated, may hold values from 0 to 31, as said below
- rel_bias: float32 [32, 16], P(None, 'tp'), may hold values from -4 to 283
- attn_gain: float32 [1024], replicated, may hold values from 0.1 to 1.9
- moe_gain: float32 [1024], replicated, may hold values from 0.1 to 1.9
- w_qkv: bfloat16 [3, 1024, 1024], P(None, None, 'tp'), may hold values from -0.1875 to 0.1875
- w_out: bfloat16 [1024, 1024], P('tp'), may hold values from -0.1875 to 0.1875
- router: bfloat16 [1024, 16], replicated, may hold values from -0.1875 to 0.1875
- expert_choice: int32 [4, 16, 2], replicated, may hold values from 0 to 15, all different within a row
- w_gate_up: bfloat16 [2, 45056, 1024], P(None, ('seq', 'tp')), may hold values from -0.1875 to 0.1875
- w_down: bfloat16 [45056, 1024], P(('seq', 'tp')), may hold values from -0.109375 to 0.109375
Outputs:
- layer_out: bfloat16 [4, 16, 1024], replicated
Inputs may be any that keep to these rules, and one draw needn't show every extreme that they name: Request r's cache holds its positions 0 to cache_len[r] - 1; some request holds exactly 2048. `bucket_table`: non-decreasing in the distance, 0 at distance 0. `expert_choice`: the 2 experts of a token differ.
All inputs are finite; a program needn't handle non-finite values.
Results may differ from a plain program's by a relative error of at most 0.012.
Values sent between devices are 32-bit elements; how exact they have to be, the bound alone decides.
No kernel may reach another device: no remote copies, remote signals or barrier semaphores. Data moves between devices by JAX's collectives and lax.ppermute only.
A program may use at most 64 MiB of HBM per device.

v0:
```python
import jax
import jax.numpy as jnp
from jax import lax
from jax.sharding import PartitionSpec as P

HEAD_DIM = 64
FF = 2816
NEG = -1e30
EPS = 1e-06


def rms_scale(values, gain_vec):
    return values * lax.rsqrt(jnp.mean(values * values, axis=-1, keepdims=True) + EPS) * gain_vec


def on_device(
    tokens_in,
    key_cache,
    value_cache,
    cache_len,
    bucket_table,
    rel_bias,
    attn_gain,
    moe_gain,
    w_qkv,
    w_out,
    router,
    expert_choice,
    w_gate_up,
    w_down,
):
    steps_all, requests, model_width = tokens_in.shape
    cache_rows = key_cache.shape[1]
    heads_local = key_cache.shape[2] // HEAD_DIM
    table_len = bucket_table.shape[0]
    num_buckets = rel_bias.shape[0]
    num_experts = router.shape[1]
    hidden_local = w_down.shape[0]
    bucket_ids = jnp.arange(num_buckets, dtype=jnp.int32)

    def bias_lookup(buckets, pattern):
        onehot = (buckets[..., None] == bucket_ids).astype(jnp.float32)
        return jnp.einsum(pattern, onehot, rel_bias, precision=lax.Precision.HIGHEST)

    normed = rms_scale(tokens_in.astype(jnp.float32), attn_gain).astype(jnp.bfloat16)
    projected = jnp.einsum(
        "srd,kdf->ksrf", normed, w_qkv, preferred_element_type=jnp.float32
    ).astype(jnp.bfloat16)
    head_shape = (steps_all, requests, heads_local, HEAD_DIM)
    queries = projected[0].reshape(head_shape)
    fresh_keys = projected[1].reshape(head_shape)
    fresh_values = projected[2].reshape(head_shape)
    keys_heads = key_cache.reshape(requests, cache_rows, heads_local, HEAD_DIM)
    values_heads = value_cache.reshape(requests, cache_rows, heads_local, HEAD_DIM)
    positions = lax.axis_index("seq") * cache_rows + jnp.arange(cache_rows, dtype=jnp.int32)
    live_rows = positions[None, :] < cache_len[:, None]

    def cache_part(query_blk, step_ids, keys_blk, vals_blk, lens_blk, live_blk):
        scores = jnp.einsum(
            "srhd,rchd->srhc", query_blk, keys_blk, preferred_element_type=jnp.float32
        )
        distance = lens_blk[None, :, None] + step_ids[:, None, None] - positions[None, None, :]
        buckets = jnp.take(bucket_table, jnp.clip(distance, 0, table_len - 1))
        scores = scores + bias_lookup(buckets, "srcb,bh->srhc")
        usable = live_blk[None, :, None, :]
        scores = jnp.where(usable, scores, NEG)
        maxima = jnp.max(scores, axis=-1)
        weights = jnp.where(usable, jnp.exp(scores - maxima[..., None]), 0.0)
        summed = jnp.einsum(
            "srhc,rchd->srhd", weights, vals_blk, preferred_element_type=jnp.float32
        )
        return (maxima, jnp.sum(weights, axis=-1), summed)

    def attend_cache(query_blk, step_ids):
        return cache_part(query_blk, step_ids, keys_heads, values_heads, cache_len, live_rows)

    def merge_cache(maxima, totals, summed):
        overall = lax.pmax(maxima, "seq")
        factor = jnp.exp(maxima - overall)
        totals, summed = lax.psum((totals * factor, summed * factor[..., None]), "seq")
        return (overall, totals, summed)

    def attend_recent(query_blk, step_ids):
        scores = jnp.einsum(
            "srhd,jrhd->srhj", query_blk, fresh_keys, preferred_element_type=jnp.float32
        )
        distance = step_ids[:, None] - jnp.arange(steps_all, dtype=jnp.int32)[None, :]
        buckets = jnp.take(bucket_table, jnp.clip(distance, 0, table_len - 1))
        scores = scores + bias_lookup(buckets, "sjb,bh->shj")[:, None]
        usable = (distance >= 0)[:, None, None, :]
        scores = jnp.where(usable, scores, NEG)
        maxima = jnp.max(scores, axis=-1)
        weights = jnp.where(usable, jnp.exp(scores - maxima[..., None]), 0.0)
        summed = jnp.einsum(
            "srhj,jrhd->srhd", weights, fresh_values, preferred_element_type=jnp.float32
        )
        return (maxima, jnp.sum(weights, axis=-1), summed)

    first_col = (lax.axis_index("seq") * lax.axis_size("tp") + lax.axis_index("tp")) * hidden_local
    col_expert = (first_col + jnp.arange(hidden_local, dtype=jnp.int32)) // FF
    owner = (col_expert[None, :] == jnp.arange(num_experts, dtype=jnp.int32)[:, None]).astype(
        jnp.float32
    )

    def layer(start, step_count):
        step_ids = jnp.arange(start, start + step_count, dtype=jnp.int32)
        query_blk = queries[start : start + step_count]
        cache_max, cache_tot, cache_sum = merge_cache(*attend_cache(query_blk, step_ids))
        new_max, new_tot, new_sum = attend_recent(query_blk, step_ids)
        joint = jnp.maximum(cache_max, new_max)
        scale_cache = jnp.exp(cache_max - joint)
        scale_new = jnp.exp(new_max - joint)
        totals = cache_tot * scale_cache + new_tot * scale_new
        summed = cache_sum * scale_cache[..., None] + new_sum * scale_new[..., None]
        attended = (
            (summed / totals[..., None])
            .reshape(step_count, requests, heads_local * HEAD_DIM)
            .astype(jnp.bfloat16)
        )
        partial_value = jnp.einsum(
            "srf,fd->srd", attended, w_out, preferred_element_type=jnp.float32
        )
        mid = tokens_in[start : start + step_count].astype(jnp.float32) + lax.psum(
            partial_value, "tp"
        )
        moe_in = rms_scale(mid, moe_gain).astype(jnp.bfloat16)
        logits = jnp.einsum("srd,de->sre", moe_in, router, preferred_element_type=jnp.float32)
        picked = expert_choice[start : start + step_count][..., None] == jnp.arange(
            num_experts, dtype=jnp.int32
        )
        chosen = jnp.sum(jnp.where(picked, logits[:, :, None, :], 0.0), axis=-1)
        leading = jax.nn.sigmoid(chosen[..., 0] - chosen[..., 1])
        gate_pair = jnp.stack([leading, 1.0 - leading], axis=-1)
        per_expert = jnp.sum(jnp.where(picked, gate_pair[..., None], 0.0), axis=2)
        coef = jnp.einsum("sre,ef->srf", per_expert, owner, precision=lax.Precision.HIGHEST)
        gate_up = jnp.einsum("srd,kfd->ksrf", moe_in, w_gate_up, preferred_element_type=jnp.float32)
        hidden = (jax.nn.gelu(gate_up[0], approximate=True) * gate_up[1] * coef).astype(
            jnp.bfloat16
        )
        expert_part = jnp.einsum("srf,fd->srd", hidden, w_down, preferred_element_type=jnp.float32)
        mixture = lax.psum(expert_part, ("seq", "tp"))
        return (mid + mixture).astype(jnp.bfloat16)

    outputs = [layer(start, 1) for start in range(steps_all)]
    return jnp.concatenate(outputs, axis=0)


def solution(mesh):
    return jax.shard_map(
        on_device,
        mesh=mesh,
        in_specs=(
            P(),
            P(None, "seq", "tp"),
            P(None, "seq", "tp"),
            P(),
            P(),
            P(None, "tp"),
            P(),
            P(),
            P(None, None, "tp"),
            P("tp", None),
            P(),
            P(),
            P(None, ("seq", "tp"), None),
            P(("seq", "tp"), None),
        ),
        out_specs=P(),
        check_vma=False,
    )
```

profile of v0, /device:TPU:0, one launch (start us, length us, event | category | flops | bytes accessed | tf_op | source)
XLA Modules:
  0.0 458.9 jit_solution(6743066980730547285)
XLA Ops:
  9.3 23.0 %gather_fusion.4 = s32[4096]{0:T(1024)S(1)} fusion(s32[2052]{0:T(1024)S(1)} %copy-done.1, s32[4096]{0:T(1024)S(1)} %broadcast_clamp_fusion.1), kind=kCustom, calls=%fused_computation.3.clone | custom fusion | bytes 49152 | tf_op jit(solution)/shard_map/jit(_take)/gather | solution.py:63
  32.4 23.0 %gather_fusion.6 = s32[4096]{0:T(1024)S(1)} fusion(s32[2052]{0:T(1024)S(1)} %copy-done.1, s32[4096]{0:T(1024)S(1)} %broadcast_clamp_fusion), kind=kCustom, calls=%fused_computation.4.clone | custom fusion | bytes 49152 | tf_op jit(solution)/shard_map/jit(_take)/gather | solution.py:63
  55.5 23.0 %gather_fusion.2 = s32[4096]{0:T(1024)S(1)} fusion(s32[2052]{0:T(1024)S(1)} %copy-done.1, s32[4096]{0:T(1024)S(1)} %broadcast_clamp_fusion.2), kind=kCustom, calls=%fused_computation.2.clone | custom fusion | bytes 49152 | tf_op jit(solution)/shard_map/jit(_take)/gather | solution.py:63
  79.3 23.0 %gather_fusion = s32[4096]{0:T(1024)S(1)} fusion(s32[2052]{0:T(1024)S(1)} %copy-done.1, s32[4096]{0:T(1024)S(1)} %broadcast_clamp_fusion.3), kind=kCustom, calls=%fused_computation.clone | custom fusion | bytes 49152 | tf_op jit(solution)/shard_map/jit(_take)/gather | solution.py:63
  103.0 1.8 fusion.9
  105.2 3.9 copy.134
  109.2 2.0 fusion.206
  112.2 2.0 fusion.205
  115.2 2.8 fusion.204
  126.0 23.4 %all-reduce.2 = (f32[1,16,4]{1,2,0:T(4,128)S(1)}, f32[1,16,4]{1,2,0:T(4,128)S(1)}, f32[1,16,4]{1,2,0:T(4,128)S(1)}, f32[1,16,4]{1,2,0:T(4,128)S(1)}) all-reduce(f32[1,16,4]{1,2,0:T(4,128)} %bitcast.599, f32[1,16,4]{1,2,0:T(4,128)} %bitcast.601, f32[1,16,4]{1,2,0:T(4,128)} %bitcast.598, ...), channel_id=1, replica_groups=mesh['seq'=8,'tp'=4] {'seq'}, use_global_device_ids=true, to_apply=%region_2.4 | all-reduce | flops 256 | bytes 2048 | tf_op jit(solution)/shard_map/pmax | solution.py:78
  152.4 3.9 copy.135
  156.4 2.4 fusion.63
  206.7 1.7 fusion.108
  208.4 1.7 fusion.106
  215.6 1.7 fusion.110
  218.7 1.7 fusion.104
  221.7 10.9 %all-reduce.10.cloned.1.call-done = (f32[1,16,4,64]{3,2,1,0:T(4,128)}, f32[1,16,4]{1,2,0:T(4,128)}, f32[1,16,4,64]{3,2,1,0:T(4,128)}, f32[1,16,4]{1,2,0:T(4,128)...) async-done(((f32[1,16,4,64]{3,2,1,0:T(4,128)}, f32[1,16,4]{1,2,0:T(4,128)}, f32[1,16,4,64]{3,2,1,0:T(4,128)}, ...) | async-done | bytes 66576 | tf_op jit(solution)/shard_map/psum | solution.py:80
  255.2 1.5 fusion.101
  268.7 30.7 %all-reduce.12.cloned.1.call-done = (f32[1,16,1024]{2,1,0:T(8,128)}, f32[1,16,1024]{2,1,0:T(8,128)}, f32[1,16,1024]{2,1,0:T(8,128)}, f32[1,16,1024]{2,1,0:T(8,128)}) async-done(((f32[1,16,1024]{2,1,0:T(8,128)}, f32[1,16,1024]{2,1,0:T(8,128)}, f32[1,16,1024]{2,1,0:T(8,128)}, f32[1,16,1024]{2,1,0:T(8,128)}), (f32[1,16,1024]{2,1,0:T(8,128)}, f32[1,16,1024]{2,1,0:T(8,128)}, f32[1,16,1024]{2,1,0:T(8,128)}, ...) | async-done | bytes 262160 | tf_op jit(solution)/shard_map/psum | solution.py:123
  303.4 4.4 fusion.95
  307.8 4.4 convolution_bitcast_fusion
  312.3 4.2 convolution_bitcast_fusion.1
  316.7 1.6 convolution_bitcast_fusion.2
  324.6 126.1 %all-reduce.8.cloned.1.call-done = (f32[1,16,1024]{2,1,0:T(8,128)}, f32[1,16,1024]{2,1,0:T(8,128)}, f32[1,16,1024]{2,1,0:T(8,128)}, f32[1,16,1024]{2,1,0:T(8,128)}) async-done(((f32[1,16,1024]{2,1,0:T(8,128)}, f32[1,16,1024]{2,1,0:T(8,128)}, f32[1,16,1024]{2,1,0:T(8,128)}, f32[1,16,1024]{2,1,0:T(8,128)}), (f32[1,16,1024]{2,1,0:T(8,128)}, f32[1,16,1024]{2,1,0:T(8,128)}, f32[1,16,1024]{2,1,0:T(8,128)}, ...) | async-done | bytes 262160 | tf_op jit(solution)/shard_map/psum | solution.py:141
  (236 shorter events, 120.4 us)
Async XLA Ops:
  6.5 313.0 %copy-start = (bf16[1408,1024]{1,0:T(8,128)(2,1)S(1)}, bf16[1408,1024]{1,0:T(8,128)(2,1)}, u32[]{:S(2)}) copy-start(bf16[1408,1024]{1,0:T(8,128)(2,1)} %param.31) | copy-start | bytes 8650756
  6.5 2.8 copy-start.1
  6.5 226.1 %all-reduce.10.cloned.1.call-start = ((), (), s32[]{:S(2)}) async-start(), calls=%async_computation.1 | async-start | bytes 278528 | tf_op jit(solution)/shard_map/psum | solution.py:80
  55.5 23.1 %copy-start.20 = (s32[16]{0:T(128)S(1)}, s32[16]{0:T(128)}, u32[]{:S(2)}) copy-start(s32[16]{0:T(128)} %param.21) | copy-start | bytes 196
  79.3 23.8 %copy-start.4 = (bf16[4,16,1024]{2,1,0:T(8,128)(2,1)S(1)}, bf16[4,16,1024]{2,1,0:T(8,128)(2,1)}, u32[]{:S(2)}) copy-start(bf16[4,16,1024]{2,1,0:T(8,128)(2,1)} %param.18) | copy-start | bytes 393220
  79.3 23.8 %copy-start.18 = (f32[1024]{0:T(1024)S(1)}, f32[1024]{0:T(1024)}, u32[]{:S(2)}) copy-start(f32[1024]{0:T(1024)} %param.24) | copy-start | bytes 12292
  115.2 2.8 copy-start.2
  115.2 3.1 copy-start.19
  149.5 2.8 copy-start.21
  149.5 2.8 copy-start.22
  152.4 3.9 copy-start.17
  156.4 3.1 copy-start.15
  160.1 11.9 %copy-start.26 = (f32[32,4]{0,1:T(4,128)S(1)}, f32[32,4]{0,1:T(4,128)}, u32[]{:S(2)}) copy-start(f32[32,4]{0,1:T(4,128)} %param.23) | copy-start | bytes 1540
  163.5 135.9 %all-reduce.12.cloned.1.call-start = ((), (), s32[]{:S(2)}) async-start(), calls=%async_computation.2 | async-start | bytes 524288 | tf_op jit(solution)/shard_map/psum | solution.py:123
  172.0 90.3 %copy-start.3 = (bf16[256,1024]{1,0:T(8,128)(2,1)S(1)}, bf16[256,1024]{1,0:T(8,128)(2,1)}, u32[]{:S(2)}) copy-start(bf16[256,1024]{1,0:T(8,128)(2,1)} %param.27) | copy-start | bytes 1572868
  173.5 10.0 %copy-start.13 = (f32[4,4]{1,0:T(4,128)}, f32[4,4]{1,0:T(4,128)S(1)}, u32[]{:S(2)}) copy-start(f32[4,4]{1,0:T(4,128)S(1)} %copy.153) | copy-start | bytes 196
  267.7 183.0 %all-reduce.8.cloned.1.call-start = ((), (), s32[]{:S(2)}) async-start(), calls=%async_computation | async-start | bytes 524288 | tf_op jit(solution)/shard_map/psum | solution.py:141
  303.4 13.3 %slice-start = ((s8[5767168]{0:T(1024)(128)(4,1)}), s8[4194304]{0:T(1024)(128)(4,1)S(1)}, s32[]{:S(2)}) async-start(s8[5767168]{0:T(1024)(128)(4,1)} %bitcast.574), calls=%async_computation.3 | async-start | bytes 8388608
  307.8 4.4 copy-start.10
  307.8 8.9 %slice-start.1 = ((s8[5767168]{0:T(1024)(128)(4,1)}), s8[1572864]{0:T(1024)(128)(4,1)S(1)}, s32[]{:S(2)}) async-start(s8[5767168]{0:T(1024)(128)(4,1)} %bitcast.574), calls=%async_computation.4 | async-start | bytes 3145728
  323.3 127.4 %copy-start.6 = (f32[1,16,1024]{2,1,0:T(8,128)S(1)}, f32[1,16,1024]{2,1,0:T(8,128)}, u32[]{:S(2)}) copy-start(f32[1,16,1024]{2,1,0:T(8,128)} %get-tuple-element.31) | copy-start | bytes 196612
  323.3 127.4 %copy-start.7 = (f32[1,16,1024]{2,1,0:T(8,128)S(1)}, f32[1,16,1024]{2,1,0:T(8,128)}, u32[]{:S(2)}) copy-start(f32[1,16,1024]{2,1,0:T(8,128)} %get-tuple-element.32) | copy-start | bytes 196612
  323.3 127.4 %copy-start.8 = (f32[1,16,1024]{2,1,0:T(8,128)S(1)}, f32[1,16,1024]{2,1,0:T(8,128)}, u32[]{:S(2)}) copy-start(f32[1,16,1024]{2,1,0:T(8,128)} %get-tuple-element.33) | copy-start | bytes 196612
  323.3 127.4 %copy-start.9 = (f32[1,16,1024]{2,1,0:T(8,128)S(1)}, f32[1,16,1024]{2,1,0:T(8,128)}, u32[]{:S(2)}) copy-start(f32[1,16,1024]{2,1,0:T(8,128)} %get-tuple-element.34) | copy-start | bytes 196612
  (8 other events, 12.1 us)
Sparse Core Ops, SparseCore 0:
  163.6 68.9 all-reduce.9
  267.8 31.5 all-reduce.11
  324.7 125.9 all-reduce.7
where the time goes:
time: 462 us; the launch traced here: 459 us
  waiting for transfers between devices  168 us (36%)
  local copies, waits for them, and re-layouts  149 us (32%)
  matrix products  57.1 us (12%)
  other arithmetic  48.1 us (10%)
  blocking collectives  23.4 us (5%)
  between operations  13.6 us (3%)
    psum x1, waiting for transfers between devices, layer(): mixture = lax.psum(expert_part, ('seq', 'tp'))  126 us
    gather x8, local copies, waits for them, and re-layouts, cache_part(): buckets = jnp.take(bucket_table, jnp.clip(distance, 0, table_len - 1))  92.2 us
    psum x1, waiting for transfers between devices, layer(): lax.psum(partial_value, 'tp')  30.7 us
    pmax x1, blocking collectives, merge_cache(): overall = lax.pmax(maxima, 'seq')  23.4 us
    dot_general x4, matrix products, layer(): jnp.einsum('srd,kfd->ksrf', moe_in, w_gate_up, preferred_element_type=jnp...  14.6 us
    psum x1, waiting for transfers between devices, merge_cache(): lax.psum((totals * factor, summed * factor[..., None]), 'seq')  10.9 us
  transfers between devices with their start and end apart: 3, of which 3 were waited for; matrix products, arithmetic and copies ran while one was open for 13% of the time, Pallas kernels for 0%

commit v1 on v0

--- a/solution.py
+++ b/solution.py
@@ -138,7 +138,8 @@
             jnp.bfloat16
         )
         expert_part = jnp.einsum("srf,fd->srd", hidden, w_down, preferred_element_type=jnp.float32)
-        mixture = lax.psum(expert_part, ("seq", "tp"))
+        partial = lax.psum(expert_part, "tp")
+        mixture = lax.psum(partial, "seq")
         return (mid + mixture).astype(jnp.bfloat16)
 
     outputs = [layer(start, 1) for start in range(steps_all)]

time: 462 us -> 444 us (0.961)
  waiting for transfers between devices: 168 us -> 149 us
    psum x1 -> x2, waiting for transfers between devices: 126 us -> 108 us  [the longest x1 75.3 us: layer(): mixture = lax.psum(partial, 'seq')]
  transfers between devices with their start and end apart: 3 -> 4, of which waited for: 3 -> 4; matrix products, arithmetic and copies ran while one was open for 13% -> 13% of each run, Pallas kernels for 0% -> 0%
where the time goes in v1:
time: 444 us; the launch traced here: 441 us
  local copies, waits for them, and re-layouts  149 us (34%)
  waiting for transfers between devices  149 us (34%)
  matrix products  57.1 us (13%)
  other arithmetic  48.1 us (11%)
  blocking collectives  23.4 us (5%)
  between operations  13.7 us (3%)
    gather x8, local copies, waits for them, and re-layouts, cache_part(): buckets = jnp.take(bucket_table, jnp.clip(distance, 0, table_len - 1))  92.2 us
    psum x1, waiting for transfers between devices, layer(): mixture = lax.psum(partial, 'seq')  75.3 us
    psum x1, waiting for transfers between devices, layer(): partial = lax.psum(expert_part, 'tp')  32.4 us
    psum x1, waiting for transfers between devices, layer(): lax.psum(partial_value, 'tp')  30.7 us
    pmax x1, blocking collectives, merge_cache(): overall = lax.pmax(maxima, 'seq')  23.4 us
    dot_general x4, matrix products, layer(): jnp.einsum('srd,kfd->ksrf', moe_in, w_gate_up, preferred_element_type=jnp...  14.6 us
    psum x1, waiting for transfers between devices, merge_cache(): lax.psum((totals * factor, summed * factor[..., None]), 'seq')  10.9 us
    unnamed x64, local copies, waits for them, and re-layouts  9.15 us
  transfers between devices with their start and end apart: 4, of which 4 were waited for; matrix products, arithmetic and copies ran while one was open for 13% of the time, Pallas kernels for 0%

profile of v1, /device:TPU:0, one launch (start us, length us, event | category | flops | bytes accessed | tf_op | source)
XLA Modules:
  0.0 440.6 jit_solution(9112296426478459819)
XLA Ops:
  9.3 23.0 %gather_fusion.4 = s32[4096]{0:T(1024)S(1)} fusion(s32[2052]{0:T(1024)S(1)} %copy-done.1, s32[4096]{0:T(1024)S(1)} %broadcast_clamp_fusion.1), kind=kCustom, calls=%fused_computation.3.clone | custom fusion | bytes 49152 | tf_op jit(solution)/shard_map/jit(_take)/gather | solution.py:63
  32.4 23.0 %gather_fusion.6 = s32[4096]{0:T(1024)S(1)} fusion(s32[2052]{0:T(1024)S(1)} %copy-done.1, s32[4096]{0:T(1024)S(1)} %broadcast_clamp_fusion), kind=kCustom, calls=%fused_computation.4.clone | custom fusion | bytes 49152 | tf_op jit(solution)/shard_map/jit(_take)/gather | solution.py:63
  55.5 23.0 %gather_fusion.2 = s32[4096]{0:T(1024)S(1)} fusion(s32[2052]{0:T(1024)S(1)} %copy-done.1, s32[4096]{0:T(1024)S(1)} %broadcast_clamp_fusion.2), kind=kCustom, calls=%fused_computation.2.clone | custom fusion | bytes 49152 | tf_op jit(solution)/shard_map/jit(_take)/gather | solution.py:63
  79.3 23.0 %gather_fusion = s32[4096]{0:T(1024)S(1)} fusion(s32[2052]{0:T(1024)S(1)} %copy-done.1, s32[4096]{0:T(1024)S(1)} %broadcast_clamp_fusion.3), kind=kCustom, calls=%fused_computation.clone | custom fusion | bytes 49152 | tf_op jit(solution)/shard_map/jit(_take)/gather | solution.py:63
  103.0 1.8 fusion.9
  105.2 3.9 copy.134
  109.2 2.0 fusion.206
  112.2 2.0 fusion.205
  115.2 2.8 fusion.204
  126.0 23.4 %all-reduce.2 = (f32[1,16,4]{1,2,0:T(4,128)S(1)}, f32[1,16,4]{1,2,0:T(4,128)S(1)}, f32[1,16,4]{1,2,0:T(4,128)S(1)}, f32[1,16,4]{1,2,0:T(4,128)S(1)}) all-reduce(f32[1,16,4]{1,2,0:T(4,128)} %bitcast.599, f32[1,16,4]{1,2,0:T(4,128)} %bitcast.601, f32[1,16,4]{1,2,0:T(4,128)} %bitcast.598, ...), channel_id=1, replica_groups=mesh['seq'=8,'tp'=4] {'seq'}, use_global_device_ids=true, to_apply=%region_2.4 | all-reduce | flops 256 | bytes 2048 | tf_op jit(solution)/shard_map/pmax | solution.py:78
  152.4 3.9 copy.135
  156.4 2.4 fusion.63
  206.7 1.7 fusion.108
  208.4 1.7 fusion.106
  215.6 1.7 fusion.110
  218.7 1.7 fusion.104
  221.7 10.9 %all-reduce.10.cloned.1.call-done = (f32[1,16,4,64]{3,2,1,0:T(4,128)}, f32[1,16,4]{1,2,0:T(4,128)}, f32[1,16,4,64]{3,2,1,0:T(4,128)}, f32[1,16,4]{1,2,0:T(4,128)...) async-done(((f32[1,16,4,64]{3,2,1,0:T(4,128)}, f32[1,16,4]{1,2,0:T(4,128)}, f32[1,16,4,64]{3,2,1,0:T(4,128)}, ...) | async-done | bytes 66576 | tf_op jit(solution)/shard_map/psum | solution.py:80
  268.7 30.7 %all-reduce.16.cloned.1.call-done = (f32[1,16,1024]{2,1,0:T(8,128)}, f32[1,16,1024]{2,1,0:T(8,128)}, f32[1,16,1024]{2,1,0:T(8,128)}, f32[1,16,1024]{2,1,0:T(8,128)}) async-done(((f32[1,16,1024]{2,1,0:T(8,128)}, f32[1,16,1024]{2,1,0:T(8,128)}, f32[1,16,1024]{2,1,0:T(8,128)}, f32[1,16,1024]{2,1,0:T(8,128)}), (f32[1,16,1024]{2,1,0:T(8,128)}, f32[1,16,1024]{2,1,0:T(8,128)}, f32[1,16,1024]{2,1,0:T(8,128)}, ...) | async-done | bytes 262160 | tf_op jit(solution)/shard_map/psum | solution.py:123
  303.4 4.4 fusion.95
  307.8 4.4 convolution_bitcast_fusion
  312.3 4.2 convolution_bitcast_fusion.1
  316.7 1.6 convolution_bitcast_fusion.2
  324.6 32.4 %all-reduce.14.cloned.1.call-done = (f32[1,16,1024]{2,1,0:T(8,128)}, f32[1,16,1024]{2,1,0:T(8,128)}, f32[1,16,1024]{2,1,0:T(8,128)}, f32[1,16,1024]{2,1,0:T(8,128)}) async-done(((f32[1,16,1024]{2,1,0:T(8,128)}, f32[1,16,1024]{2,1,0:T(8,128)}, f32[1,16,1024]{2,1,0:T(8,128)}, f32[1,16,1024]{2,1,0:T(8,128)}), (f32[1,16,1024]{2,1,0:T(8,128)}, f32[1,16,1024]{2,1,0:T(8,128)}, f32[1,16,1024]{2,1,0:T(8,128)}, ...) | async-done | bytes 262160 | tf_op jit(solution)/shard_map/psum | solution.py:141
  357.1 75.3 %all-reduce.12.cloned.1.call-done = (f32[1,16,1024]{2,1,0:T(8,128)}, f32[1,16,1024]{2,1,0:T(8,128)}, f32[1,16,1024]{2,1,0:T(8,128)}, f32[1,16,1024]{2,1,0:T(8,128)}) async-done(((f32[1,16,1024]{2,1,0:T(8,128)}, f32[1,16,1024]{2,1,0:T(8,128)}, f32[1,16,1024]{2,1,0:T(8,128)}, f32[1,16,1024]{2,1,0:T(8,128)}), (f32[1,16,1024]{2,1,0:T(8,128)}, f32[1,16,1024]{2,1,0:T(8,128)}, f32[1,16,1024]{2,1,0:T(8,128)}, ...) | async-done | bytes 262160 | tf_op jit(solution)/shard_map/psum | solution.py:142
  (239 shorter events, 122.0 us)
Async XLA Ops:
  6.5 313.0 %copy-start = (bf16[1408,1024]{1,0:T(8,128)(2,1)S(1)}, bf16[1408,1024]{1,0:T(8,128)(2,1)}, u32[]{:S(2)}) copy-start(bf16[1408,1024]{1,0:T(8,128)(2,1)} %param.31) | copy-start | bytes 8650756
  6.5 2.8 copy-start.1
  6.5 226.1 %all-reduce.10.cloned.1.call-start = ((), (), s32[]{:S(2)}) async-start(), calls=%async_computation | async-start | bytes 278528 | tf_op jit(solution)/shard_map/psum | solution.py:80
  55.5 23.1 %copy-start.20 = (s32[16]{0:T(128)S(1)}, s32[16]{0:T(128)}, u32[]{:S(2)}) copy-start(s32[16]{0:T(128)} %param.21) | copy-start | bytes 196
  79.3 23.8 %copy-start.4 = (bf16[4,16,1024]{2,1,0:T(8,128)(2,1)S(1)}, bf16[4,16,1024]{2,1,0:T(8,128)(2,1)}, u32[]{:S(2)}) copy-start(bf16[4,16,1024]{2,1,0:T(8,128)(2,1)} %param.18) | copy-start | bytes 393220
  79.3 23.8 %copy-start.18 = (f32[1024]{0:T(1024)S(1)}, f32[1024]{0:T(1024)}, u32[]{:S(2)}) copy-start(f32[1024]{0:T(1024)} %param.24) | copy-start | bytes 12292
  115.2 3.1 copy-start.19
  149.5 2.8 copy-start.21
  149.5 2.8 copy-start.22
  152.4 3.9 copy-start.17
  156.4 3.1 copy-start.15
  160.1 11.9 %copy-start.26 = (f32[32,4]{0,1:T(4,128)S(1)}, f32[32,4]{0,1:T(4,128)}, u32[]{:S(2)}) copy-start(f32[32,4]{0,1:T(4,128)} %param.23) | copy-start | bytes 1540
  163.5 135.9 %all-reduce.16.cloned.1.call-start = ((), (), s32[]{:S(2)}) async-start(), calls=%async_computation.3 | async-start | bytes 524288 | tf_op jit(solution)/shard_map/psum | solution.py:123
  172.0 90.3 %copy-start.3 = (bf16[256,1024]{1,0:T(8,128)(2,1)S(1)}, bf16[256,1024]{1,0:T(8,128)(2,1)}, u32[]{:S(2)}) copy-start(bf16[256,1024]{1,0:T(8,128)(2,1)} %param.27) | copy-start | bytes 1572868
  173.5 10.0 %copy-start.13 = (f32[4,4]{1,0:T(4,128)}, f32[4,4]{1,0:T(4,128)S(1)}, u32[]{:S(2)}) copy-start(f32[4,4]{1,0:T(4,128)S(1)} %copy.153) | copy-start | bytes 196
  267.7 89.3 %all-reduce.14.cloned.1.call-start = ((), (), s32[]{:S(2)}) async-start(), calls=%async_computation.2 | async-start | bytes 524288 | tf_op jit(solution)/shard_map/psum | solution.py:141
  303.4 13.3 %slice-start = ((s8[5767168]{0:T(1024)(128)(4,1)}), s8[4194304]{0:T(1024)(128)(4,1)S(1)}, s32[]{:S(2)}) async-start(s8[5767168]{0:T(1024)(128)(4,1)} %bitcast.574), calls=%async_computation.4 | async-start | bytes 8388608
  307.8 4.4 copy-start.10
  307.8 8.9 %slice-start.1 = ((s8[5767168]{0:T(1024)(128)(4,1)}), s8[1572864]{0:T(1024)(128)(4,1)S(1)}, s32[]{:S(2)}) async-start(s8[5767168]{0:T(1024)(128)(4,1)} %bitcast.574), calls=%async_computation.5 | async-start | bytes 3145728
  323.3 109.1 %copy-start.6 = (f32[1,16,1024]{2,1,0:T(8,128)S(1)}, f32[1,16,1024]{2,1,0:T(8,128)}, u32[]{:S(2)}) copy-start(f32[1,16,1024]{2,1,0:T(8,128)} %get-tuple-element.35) | copy-start | bytes 196612
  323.3 109.1 %copy-start.7 = (f32[1,16,1024]{2,1,0:T(8,128)S(1)}, f32[1,16,1024]{2,1,0:T(8,128)}, u32[]{:S(2)}) copy-start(f32[1,16,1024]{2,1,0:T(8,128)} %get-tuple-element.36) | copy-start | bytes 196612
  323.3 109.1 %copy-start.8 = (f32[1,16,1024]{2,1,0:T(8,128)S(1)}, f32[1,16,1024]{2,1,0:T(8,128)}, u32[]{:S(2)}) copy-start(f32[1,16,1024]{2,1,0:T(8,128)} %get-tuple-element.37) | copy-start | bytes 196612
  323.3 109.1 %copy-start.9 = (f32[1,16,1024]{2,1,0:T(8,128)S(1)}, f32[1,16,1024]{2,1,0:T(8,128)}, u32[]{:S(2)}) copy-start(f32[1,16,1024]{2,1,0:T(8,128)} %get-tuple-element.38) | copy-start | bytes 196612
  324.6 107.8 %all-reduce.12.cloned.1.call-start = ((), (), s32[]{:S(2)}) async-start(), calls=%async_computation.1 | async-start | bytes 524288 | tf_op jit(solution)/shard_map/psum | solution.py:142
  (9 other events, 14.8 us)
Sparse Core Ops, SparseCore 0:
  163.6 68.9 all-reduce.9
  267.8 31.5 all-reduce.15
  324.7 32.2 all-reduce.13
  361.0 71.2 all-reduce.11
